TPU v7x, 256 devices: a whole 4x4x8 slice. The times are simulated.
256 devices in a mesh: col: 16 (over z, core), row: 16 (over x, y).
Axes of the slice: x: 4, y: 4, z: 8, core: 2. Of those that a mesh axis runs over, the one named last changes fastest.
Arguments:
- lower_cols: float32 [4096, 2048], P('col', 'row'), may hold values from -6 to 6
- pivot_rows: float32 [8192, 4096], P('row', 'col')
- pattern: int32 [64, 32], replicated, may hold values 0 or 1
- panel_in: float32 [8192, 2048], P('col', 'row'), may hold values from -6 to 6
- diag_in: float32 [64, 128, 128], P('col'), as said below
Outputs:
- panel: float32 [8192, 2048], P('col', 'row')
- factor: float32 [64, 128, 128], P('col')
Inputs may be any that keep to these rules, and one draw needn't show every extreme that they name: diag_in holds symmetric blocks with diagonal entries between 2.5 and 4.5; diag_in[j] - dsum[j] is positive definite.
All inputs are finite; a program needn't handle non-finite values.
Results may differ from a plain program's by a relative error of at most 0.00005.
Values sent between devices are 32-bit elements; how exact they have to be, the bound alone decides.
A program may use at most 128 MiB of HBM per device.

v0:
```python
import jax
import jax.numpy as jnp
from jax import lax
from jax.sharding import PartitionSpec as P

B = 128


def shards(lower_cols, pivot_rows, pattern, panel_in, diag_in):
    col_index = lax.axis_index("col")
    k_local = lower_cols.shape[0] // B
    targets = pattern.shape[0]
    own_targets = diag_in.shape[0]
    width = panel_in.shape[1]
    whole_pivot = lax.all_gather(pivot_rows, "row", axis=0, tiled=True)
    local_pattern = lax.dynamic_slice_in_dim(pattern, col_index * k_local, k_local, 1).astype(
        jnp.float32
    )
    masked = whole_pivot.reshape(targets, B, k_local, B) * local_pattern[:, None, :, None]
    masked = masked.reshape(targets * B, k_local * B)
    update = lax.psum_scatter(
        jnp.dot(
            masked, lower_cols, precision=lax.Precision.HIGHEST, preferred_element_type=jnp.float32
        ),
        "col",
        scatter_dimension=0,
        tiled=True,
    )
    blocks = masked.reshape(targets, B, k_local * B)
    partial_diag = jnp.einsum("jak,jbk->jab", blocks, blocks, precision=lax.Precision.HIGHEST)
    dsum = lax.psum_scatter(partial_diag, "col", scatter_dimension=0, tiled=True)
    factor = jnp.linalg.cholesky(diag_in - dsum)
    residue = (panel_in - update).reshape(own_targets, B, width)
    solved = lax.linalg.triangular_solve(factor, residue, left_side=True, lower=True)
    return (solved.reshape(own_targets * B, width), factor)


def solution(mesh):
    in_specs = (P("col", "row"), P("row", "col"), P(), P("col", "row"), P("col", None, None))
    out_specs = (P("col", "row"), P("col", None, None))
    return jax.shard_map(shards, mesh=mesh, in_specs=in_specs, out_specs=out_specs, check_vma=False)
```

profile of v0, /device:TPU:2, one launch (start us, length us, event | category | flops | bytes accessed | tf_op | source)
XLA Modules:
  0.0 266.4 jit_solution(10246708308004626296)
XLA Ops:
  7.2 0.0 copy-start
  7.2 0.0 all-gather.2.cloned.1.call-start
  7.2 0.7 all-gather.2.cloned.1.call-update
  7.9 0.0 reduce-scatter.3.cloned.1.call-start
  8.0 0.7 dynamic-slice_convert_fusion
  8.7 0.1 copy.13
  8.8 0.1 mul.24
  8.9 80.3 %all-gather.2.cloned.1.call-done = f32[8192,256]{1,0:T(8,128)} async-done(((f32[512,256]{1,0:T(8,128)}), f32[8192,256]{1,0:T(8,128)}) %all-gather.2.cloned.1.call-update) | async-done | bytes 8388624 | tf_op jit(solution)/shard_map/all_gather | solution.py:15
  89.2 16.6 %fusion.2 = f32[64,128,128]{1,2,0:T(8,128)} fusion(f32[64,128,256]{2,1,0:T(8,128)} %bitcast.23, f32[64,256]{1,0:T(8,128)S(1)} %bitcast.26), kind=kOutput, calls=%fused_computation.3 | convolution fusion | flops 3223322624 | bytes 12648448 | tf_op jit(solution)/shard_map/jak,jbk->jab/dot_general | solution.py:30
  105.8 0.0 reduce-scatter.3.cloned.1.call-update
  105.9 0.0 reduce-scatter.5.cloned.1.call-start
  105.9 5.4 %mul.28 = f32[64,128,2,128]{3,2,1,0:T(2,128)} broadcast(f32[64,2]{1,0:T(8,128)S(1)} %copy.13), dimensions={0,2} | broadcast | bytes 8389120 | tf_op jit(solution)/shard_map/mul | solution.py:19
  111.3 0.0 copy-done
  111.3 0.0 copy-start.2
  111.3 0.0 copy-start.1
  111.3 12.2 %fusion = f32[8192,128]{1,0:T(8,128)} fusion(f32[256,128]{1,0:T(8,128)S(1)} %copy-done, f32[8192,256]{1,0:T(8,128)} %all-gather.2.cloned.1.call-done, f32[1024,8,2,128]{3,2,1,0:T(2,128)} %bitcast.24), kind=kOutput, calls=%fused_computation.1 | convolution fusion | flops 3223322624 | bytes 21102592 | tf_op jit(solution)/shard_map/dot_general | solution.py:22
  123.5 0.0 reduce-scatter.5.cloned.1.call-update
  123.6 0.0 copy-done.2
  123.6 0.1 copy.15
  123.8 45.4 %reduce-scatter.3.cloned.1.call-done = f32[4,128,128]{1,2,0:T(8,128)} async-done(((f32[64,128,128]{1,2,0:T(8,128)}), f32[4,128,128]{1,2,0:T(8,128)}) %reduce-scatter.3.cloned.1.call-update) | async-done | bytes 262160 | tf_op jit(solution)/shard_map/reduce_scatter | solution.py:31
  169.2 1.0 sub.6
  170.2 0.1 copy.16
  170.3 46.9 %custom-call.7 = f32[4,128,128]{2,1,0:T(8,128)S(1)} custom-call(f32[4,128,128]{2,1,0:T(8,128)S(1)} %fusion.7), custom_call_target="Cholesky" | custom-call | tf_op jit(solution)/shard_map/jit(cholesky)/cholesky | solution.py:32
  217.3 0.1 compare_reduce_fusion
  217.4 0.8 select_bitcast_fusion
  218.2 39.3 %custom-call.8 = f32[4,1,128,128]{2,3,1,0:T(8,128)S(1)} custom-call(f32[4,1,128,128]{3,2,1,0:T(8,128)S(1)} %get-tuple-element.2), custom_call_target="InvertDiagBlocksLowerTriangular" | custom-call | tf_op jit(solution)/shard_map/triangular_solve | solution.py:34
  257.5 0.0 reduce-scatter.5.cloned.1.call-done
  257.5 0.0 copy-done.1
  257.6 1.0 sub.7
  258.5 1.3 fusion.5
  (5 shorter events, 0.1 us)
Async XLA Ops:
  7.2 104.2 %copy-start = (f32[256,128]{1,0:T(8,128)S(1)}, f32[256,128]{1,0:T(8,128)}, u32[]{:S(2)}) copy-start(f32[256,128]{1,0:T(8,128)} %param.5) | copy-start | bytes 393220
  7.2 82.0 %all-gather.2.cloned.1.call-start = ((), (), s32[]{:S(2)}) async-start(), calls=%async_computation.2 | async-start | bytes 8912896 | tf_op jit(solution)/shard_map/all_gather | solution.py:15
  7.9 161.3 %reduce-scatter.3.cloned.1.call-start = ((), (), s32[]{:S(2)}) async-start(), calls=%async_computation.3 | async-start | bytes 4456448 | tf_op jit(solution)/shard_map/reduce_scatter | solution.py:31
  105.9 151.7 %reduce-scatter.5.cloned.1.call-start = ((), (), s32[]{:S(2)}) async-start(), calls=%async_computation.4 | async-start | bytes 4456448 | tf_op jit(solution)/shard_map/reduce_scatter | solution.py:21
  111.3 12.2 %copy-start.2 = (f32[4,128,128]{2,1,0:T(8,128)S(1)}, f32[4,128,128]{2,1,0:T(8,128)}, u32[]{:S(2)}) copy-start(f32[4,128,128]{2,1,0:T(8,128)} %param.9) | copy-start | bytes 786436
  111.3 146.2 %copy-start.1 = (f32[512,128]{1,0:T(8,128)S(1)}, f32[512,128]{1,0:T(8,128)}, u32[]{:S(2)}) copy-start(f32[512,128]{1,0:T(8,128)} %param.8) | copy-start | bytes 786436
Sparse Core Ops, SparseCore 0:
  10.4 78.7 all-gather.1
  106.0 63.1 reduce-scatter.2
  171.7 62.2 reduce-scatter.4
where the time goes:
time: 267 us; the launch traced here: 266 us
  waiting for transfers between devices  126 us (47%)
  other arithmetic  89.9 us (34%)
  matrix products  30.1 us (11%)
  between operations  13.9 us (5%)
  local copies, waits for them, and re-layouts  5.94 us (2%)
    all_gather x1, waiting for transfers between devices, shards(): whole_pivot = lax.all_gather(pivot_rows, 'row', axis=0, tiled=True)  80.3 us
    another operation x4, other arithmetic, shards(): factor = jnp.linalg.cholesky(diag_in - dsum)  47.1 us
    reduce_scatter x1, waiting for transfers between devices, shards(): lax.psum_scatter(partial_diag, 'col', scatter_dimension=0, tiled=True)  45.4 us
    another operation x3, other arithmetic, shards(): lax.linalg.triangular_solve(factor, residue, left_side=True, lower=True)  40.1 us
    dot_general x1, matrix products, shards(): jnp.einsum('jak,jbk->jab', blocks, blocks, precision=lax.Precision.HIGHEST)  16.6 us
    dot_general x1, matrix products, shards(): jnp.dot(masked, lower_cols, precision=lax.Precision.HIGHEST, preferred_el...  12.2 us
    mul x2, local copies, waits for them, and re-layouts, shards(): whole_pivot.reshape(targets, B, k_local, B)  5.56 us
  transfers between devices with their start and end apart: 3, of which 2 were waited for; matrix products, arithmetic and copies ran while one was open for 40% of the time, Pallas kernels for 0%

commit v1 on v0

--- a/solution.py
+++ b/solution.py
@@ -1,3 +1,4 @@
+import functools
 import jax
 import jax.numpy as jnp
 from jax import lax
@@ -6,13 +7,29 @@
 B = 128
 
 
+def build_clusters(array_in, dim_k):
+    val = jnp.concatenate(
+        lax.all_to_all(
+            jnp.stack([array_in] * lax.axis_size("row"), axis=0),
+            axis_name="row",
+            split_axis=0,
+            concat_axis=0,
+        ),
+        dim_k,
+    )
+    return val
+
+
+name_run_here = functools.partial(build_clusters, dim_k=0)
+
+
 def shards(lower_cols, pivot_rows, pattern, panel_in, diag_in):
     col_index = lax.axis_index("col")
     k_local = lower_cols.shape[0] // B
     targets = pattern.shape[0]
     own_targets = diag_in.shape[0]
     width = panel_in.shape[1]
-    whole_pivot = lax.all_gather(pivot_rows, "row", axis=0, tiled=True)
+    whole_pivot = name_run_here(pivot_rows)
     local_pattern = lax.dynamic_slice_in_dim(pattern, col_index * k_local, k_local, 1).astype(
         jnp.float32
     )

time: 267 us -> 350 us (1.31)
  waiting for transfers between devices: 126 us -> 197 us
  starting transfers between devices: 0.12 us -> 7.56 us
  local copies, waits for them, and re-layouts: 5.94 us -> 11 us
    all_to_all x0 -> x1, waiting for transfers between devices: none -> 104 us  [build_clusters(): lax.all_to_all(jnp.stack([array_in] * lax.axis_size('row'), axis=0), axis...]
    all_gather x1 -> x0, waiting for transfers between devices: 80.3 us -> none  [shards(): whole_pivot = lax.all_gather(pivot_rows, 'row', axis=0, tiled=True)]
    reduce_scatter x1, waiting for transfers between devices: 45.4 us -> 93.1 us  [shards(): lax.psum_scatter(partial_diag, 'col', scatter_dimension=0, tiled=True)]
    all_to_all x0 -> x1, starting transfers between devices: none -> 7.48 us  [build_clusters(): lax.all_to_all(jnp.stack([array_in] * lax.axis_size('row'), axis=0), axis...]
    another operation x0 -> x1, local copies, waits for them, and re-layouts: none -> 5.1 us  [build_clusters(): jnp.stack([array_in] * lax.axis_size('row'), axis=0)]
  transfers between devices with their start and end apart: 3 -> 3, of which waited for: 2 -> 2; matrix products, arithmetic and copies ran while one was open for 40% -> 31% of each run, Pallas kernels for 0% -> 0%
where the time goes in v1:
time: 350 us
  waiting for transfers between devices  197 us (56%)
  other arithmetic  89.9 us (26%)
  matrix products  30.1 us (9%)
  between operations  14.1 us (4%)
  local copies, waits for them, and re-layouts  11 us (3%)
  starting transfers between devices  7.56 us (2%)
    all_to_all x1, waiting for transfers between devices, build_clusters(): lax.all_to_all(jnp.stack([array_in] * lax.axis_size('row'), axis=0), axis...  104 us
    reduce_scatter x1, waiting for transfers between devices, shards(): lax.psum_scatter(partial_diag, 'col', scatter_dimension=0, tiled=True)  93.1 us
    another operation x4, other arithmetic, shards(): factor = jnp.linalg.cholesky(diag_in - dsum)  47.1 us
    another operation x3, other arithmetic, shards(): lax.linalg.triangular_solve(factor, residue, left_side=True, lower=True)  40.1 us
    dot_general x1, matrix products, shards(): jnp.einsum('jak,jbk->jab', blocks, blocks, precision=lax.Precision.HIGHEST)  16.6 us
    dot_general x1, matrix products, shards(): jnp.dot(masked, lower_cols, precision=lax.Precision.HIGHEST, preferred_el...  12.2 us
    all_to_all x1, starting transfers between devices, build_clusters(): lax.all_to_all(jnp.stack([array_in] * lax.axis_size('row'), axis=0), axis...  7.48 us
  transfers between devices with their start and end apart: 3, of which 2 were waited for; matrix products, arithmetic and copies ran while one was open for 31% of the time, Pallas kernels for 0%

profile of v1, /device:TPU:2, one launch (start us, length us, event | category | flops | bytes accessed | tf_op | source)
XLA Modules:
  0.0 349.7 jit_solution(5366923718302260636)
XLA Ops:
  7.2 0.0 copy-start
  7.2 5.1 %stack.2 = f32[16,512,256]{2,1,0:T(8,128)} broadcast(f32[512,256]{1,0:T(8,128)} %param.6), dimensions={1,2} | broadcast | bytes 8912896 | tf_op jit(solution)/shard_map/stack | solution.py:13
  12.3 7.5 %all-to-all-start = ((f32[16,512,256]{2,1,0:T(8,128)}), f32[16,512,256]{2,1,0:T(8,128)}, u32[]{:S(2)}, u32[]{:S(2)}) async-start(f32[16,512,256]{2,1,0:T(8,128)} %stack.2), calls=%async_computation | async-start | bytes 16777216 | tf_op jit(solution)/shard_map/all_to_all | solution.py:12
  19.8 0.0 reduce-scatter.3.cloned.1.call-start
  19.8 0.7 dynamic-slice_convert_fusion
  20.5 0.1 copy.13
  20.6 0.1 mul.24
  20.7 103.8 %all-to-all-done = f32[16,512,256]{2,1,0:T(8,128)} async-done(((f32[16,512,256]{2,1,0:T(8,128)}), f32[16,512,256]{2,1,0:T(8,128)}, u32[]{:S(2)}, u32[]{:S(2)}) %all-to-all-start) | async-done | bytes 8388640 | tf_op jit(solution)/shard_map/all_to_all | solution.py:12
  124.6 16.6 %fusion.2 = f32[64,128,128]{1,2,0:T(8,128)} fusion(f32[64,128,256]{2,1,0:T(8,128)} %bitcast, f32[64,256]{1,0:T(8,128)S(1)} %bitcast.26), kind=kOutput, calls=%fused_computation.3 | convolution fusion | flops 3223322624 | bytes 12648448 | tf_op jit(solution)/shard_map/jak,jbk->jab/dot_general | solution.py:47
  141.2 0.0 reduce-scatter.3.cloned.1.call-update
  141.2 0.0 reduce-scatter.5.cloned.1.call-start
  141.3 5.4 %mul.28 = f32[64,128,2,128]{3,2,1,0:T(2,128)} broadcast(f32[64,2]{1,0:T(8,128)S(1)} %copy.13), dimensions={0,2} | broadcast | bytes 8389120 | tf_op jit(solution)/shard_map/mul | solution.py:36
  146.7 0.0 copy-done
  146.7 0.0 copy-start.2
  146.7 0.0 copy-start.1
  146.7 12.2 %fusion = f32[8192,128]{1,0:T(8,128)} fusion(f32[256,128]{1,0:T(8,128)S(1)} %copy-done, f32[8192,256]{1,0:T(8,128)} %bitcast.4, f32[1024,8,2,128]{3,2,1,0:T(2,128)} %bitcast.24), kind=kOutput, calls=%fused_computation.1 | convolution fusion | flops 3223322624 | bytes 21102592 | tf_op jit(solution)/shard_map/dot_general | solution.py:39
  158.9 0.0 reduce-scatter.5.cloned.1.call-update
  158.9 0.0 copy-done.2
  158.9 0.1 copy.15
  159.1 93.1 %reduce-scatter.3.cloned.1.call-done = f32[4,128,128]{1,2,0:T(8,128)} async-done(((f32[64,128,128]{1,2,0:T(8,128)}), f32[4,128,128]{1,2,0:T(8,128)}) %reduce-scatter.3.cloned.1.call-update) | async-done | bytes 262160 | tf_op jit(solution)/shard_map/reduce_scatter | solution.py:48
  252.2 1.0 sub.6
  253.2 0.1 copy.16
  253.4 46.9 %custom-call.7 = f32[4,128,128]{2,1,0:T(8,128)S(1)} custom-call(f32[4,128,128]{2,1,0:T(8,128)S(1)} %fusion.7), custom_call_target="Cholesky" | custom-call | tf_op jit(solution)/shard_map/jit(cholesky)/cholesky | solution.py:49
  300.3 0.1 compare_reduce_fusion
  300.4 0.8 select_bitcast_fusion
  301.3 39.3 %custom-call.8 = f32[4,1,128,128]{2,3,1,0:T(8,128)S(1)} custom-call(f32[4,1,128,128]{3,2,1,0:T(8,128)S(1)} %get-tuple-element.2), custom_call_target="InvertDiagBlocksLowerTriangular" | custom-call | tf_op jit(solution)/shard_map/triangular_solve | solution.py:51
  340.6 0.0 reduce-scatter.5.cloned.1.call-done
  340.6 0.0 copy-done.1
  340.6 1.0 sub.7
  341.6 1.3 fusion.5
  (5 shorter events, 0.1 us)
Async XLA Ops:
  7.2 139.5 %copy-start = (f32[256,128]{1,0:T(8,128)S(1)}, f32[256,128]{1,0:T(8,128)}, u32[]{:S(2)}) copy-start(f32[256,128]{1,0:T(8,128)} %param.5) | copy-start | bytes 393220
  12.3 112.3 %all-to-all-start = ((f32[16,512,256]{2,1,0:T(8,128)}), f32[16,512,256]{2,1,0:T(8,128)}, u32[]{:S(2)}, u32[]{:S(2)}) async-start(f32[16,512,256]{2,1,0:T(8,128)} %stack.2), calls=%async_computation | async-start | bytes 16777216 | tf_op jit(solution)/shard_map/all_to_all | solution.py:12
  19.8 232.5 %reduce-scatter.3.cloned.1.call-start = ((), (), s32[]{:S(2)}) async-start(), calls=%async_computation.3 | async-start | bytes 4456448 | tf_op jit(solution)/shard_map/reduce_scatter | solution.py:48
  141.2 199.4 %reduce-scatter.5.cloned.1.call-start = ((), (), s32[]{:S(2)}) async-start(), calls=%async_computation.4 | async-start | bytes 4456448 | tf_op jit(solution)/shard_map/reduce_scatter | solution.py:38
  146.7 12.2 %copy-start.2 = (f32[4,128,128]{2,1,0:T(8,128)S(1)}, f32[4,128,128]{2,1,0:T(8,128)}, u32[]{:S(2)}) copy-start(f32[4,128,128]{2,1,0:T(8,128)} %param.9) | copy-start | bytes 786436
  146.7 193.9 %copy-start.1 = (f32[512,128]{1,0:T(8,128)S(1)}, f32[512,128]{1,0:T(8,128)}, u32[]{:S(2)}) copy-start(f32[512,128]{1,0:T(8,128)} %param.8) | copy-start | bytes 786436
Sparse Core Ops, SparseCore 0:
  141.3 110.8 reduce-scatter.2
  254.8 62.3 reduce-scatter.4
